TPU v7x, 32 devices: a whole 2x2x4 slice. The times are simulated.
32 devices in a mesh: dp: 4 (over z), tensor: 8 (over y, x, core).
Axes of the slice: x: 2, y: 2, z: 4, core: 2. Of those that a mesh axis runs over, the one named last changes fastest.
Arguments:
- activations: bfloat16 [3072, 4096], P('dp', 'tensor'), may hold values from -6 to 6
- out_grads_t: bfloat16 [5504, 3072], P('tensor', 'dp'), may hold values from -6 to 6
- in_basis: bfloat16 [4096, 4096], P(None, 'tensor'), may hold values from -0.09375 to 0.09375
- out_basis_t: bfloat16 [5504, 5504], P('tensor'), may hold values from -0.078125 to 0.078125
- query_proj: bfloat16 [4, 5504, 4096], P(None, 'tensor', 'dp'), may hold values from -6 to 6
- eigvals: float32 [5504, 4096], P('tensor', 'dp'), may hold values from 0.05 to 5
- damping: float32 [1], replicated, may hold values from 0.05 to 0.2
- lengths: int32 [24], P('dp'), may hold values from 1 to 128, 1920 in all
Outputs:
- scores: float32 [24, 4], P('dp')
Inputs may be any that keep to these rules, and one draw needn't show every extreme that they name: `lengths`: the largest token count is exactly 128.
All inputs are finite; a program needn't handle non-finite values. No bound on the sum of `lengths` on one device may be relied on, other than what follows from the above.
Results may differ from a plain program's by a relative error of at most 0.006.
Values may be sent and summed in bfloat16 or wider, within the bound.
A program may use at most 128 MiB of HBM per device.

v0:
```python
import jax
import jax.numpy as jnp
from jax import lax
from jax.sharding import PartitionSpec as P


def local(activations, out_grads_t, in_basis, out_basis_t, query_proj, eigvals, damping, lengths):
    full_act = lax.all_gather(activations, "tensor", axis=1, tiled=True)
    act_local = jnp.dot(full_act, in_basis, preferred_element_type=jnp.float32).astype(jnp.bfloat16)
    act_proj = lax.all_gather(act_local, "tensor", axis=1, tiled=True)
    token_rows = full_act.shape[0]
    width = out_basis_t.shape[0]
    grad_full = jnp.dot(
        out_basis_t,
        lax.all_gather(out_grads_t, "tensor", axis=0, tiled=True),
        preferred_element_type=jnp.float32,
    )
    seq_count = lengths.shape[0]
    seq_len = token_rows // seq_count
    position = lax.broadcasted_iota(jnp.int32, (seq_count, seq_len), 1)
    keep = (position < lengths[:, None]).astype(jnp.float32).reshape(1, token_rows)
    grad_proj = (grad_full * keep).astype(jnp.bfloat16)
    scaled = (query_proj.astype(jnp.float32) / (eigvals + damping[0])).astype(jnp.bfloat16)
    query_count = query_proj.shape[0]
    mixed = jnp.einsum(
        "td,qjd->qjt",
        act_proj,
        lax.all_gather(scaled, "dp", axis=2, tiled=True),
        preferred_element_type=jnp.float32,
    )
    weighted = mixed * grad_proj.astype(jnp.float32)[None, :, :]
    partial_value = jnp.sum(weighted.reshape(query_count, width, seq_count, seq_len), axis=(1, 3)).T
    totals = lax.psum(partial_value, "tensor")
    norm_factor = (act_proj.shape[1] * out_basis_t.shape[1] * seq_len) ** (-0.5)
    return totals * norm_factor


def solution(mesh):
    placed = (
        P("dp", "tensor"),
        P("tensor", "dp"),
        P(None, "tensor"),
        P("tensor", None),
        P(None, "tensor", "dp"),
        P("tensor", "dp"),
        P(),
        P("dp"),
    )
    return jax.shard_map(
        local, mesh=mesh, in_specs=placed, out_specs=P("dp", None), check_vma=False
    )
```

profile of v0, /device:TPU:0, one launch (start us, length us, event | category | flops | bytes accessed | tf_op | source)
XLA Modules:
  0.0 591.1 jit_solution(7677577895891891836)
XLA Ops:
  6.5 0.0 all-gather.7.cloned.1.call-start
  6.5 0.7 all-gather.7.cloned.1.call-update
  7.3 0.0 all-gather.11.cloned.1.call-start
  7.3 0.7 all-gather.11.cloned.1.call-update
  8.0 0.0 copy-start
  8.0 0.0 all-gather.9.cloned.1.call-start
  8.1 50.5 %all-gather.7.cloned.1.call-done = bf16[768,4096]{1,0:T(8,128)(2,1)} async-done(((bf16[768,512]{1,0:T(8,128)(2,1)}), bf16[768,4096]{1,0:T(8,128)(2,1)}) %all-gather.7.cloned.1.call-update) | async-done | bytes 6291472 | tf_op jit(solution)/shard_map/all_gather | solution.py:8
  58.5 8.3 %convolution_convert_fusion = bf16[768,512]{1,0:T(8,128)(2,1)} fusion(bf16[768,4096]{1,0:T(8,128)(2,1)} %all-gather.7.cloned.1.call-done, bf16[4096,512]{1,0:T(8,128)(2,1)} %param.10), kind=kOutput, calls=%fused_computation.7 | convolution fusion | flops 3221618688 | bytes 11272192 | tf_op jit(solution)/shard_map/dot_general | solution.py:9
  66.9 0.0 all-gather.9.cloned.1.call-update
  66.9 0.0 all-gather.5.cloned.1.call-start
  67.6 0.0 copy-done
  67.6 0.5 broadcast_add_fusion
  68.1 0.0 copy-start.1
  68.1 7.5 %divide_convert_fusion = bf16[4,688,1024]{2,1,0:T(8,128)(2,1)} fusion(bf16[4,688,1024]{2,1,0:T(8,128)(2,1)} %param.12, f32[688,1024]{1,0:T(8,128)S(1)} %broadcast_add_fusion), kind=kLoop, calls=%fused_computation | loop fusion | flops 8454144 | bytes 14090240 | tf_op jit(solution)/shard_map/convert_element_type | solution.py:23
  75.6 0.0 all-gather.5.cloned.1.call-update
  75.6 0.0 copy-done.1
  75.6 0.1 convert_bitcast_fusion
  75.7 39.3 %all-gather.11.cloned.1.call-done = bf16[5504,768]{1,0:T(8,128)(2,1)} async-done(((bf16[688,768]{1,0:T(8,128)(2,1)}), bf16[5504,768]{1,0:T(8,128)(2,1)}) %all-gather.11.cloned.1.call-update) | async-done | bytes 8454160 | tf_op jit(solution)/shard_map/all_gather | solution.py:15
  115.0 10.9 %fusion.4 = f32[688,768]{1,0:T(8,128)S(1)} fusion(bf16[688,5504]{1,0:T(8,128)(2,1)} %param.11, bf16[5504,768]{1,0:T(8,128)(2,1)} %all-gather.11.cloned.1.call-done, f32[768]{0:T(1024)S(1)} %convert_bitcast_fusion), kind=kOutput, calls=%fused_computation.5 | convolution fusion | flops 5818036224 | bytes 18144256 | tf_op jit(solution)/shard_map/dot_general | solution.py:13
  125.9 37.6 %all-gather.9.cloned.1.call-done = bf16[768,4096]{1,0:T(8,128)(2,1)} async-done(((bf16[768,512]{1,0:T(8,128)(2,1)}), bf16[768,4096]{1,0:T(8,128)(2,1)}) %all-gather.9.cloned.1.call-update) | async-done | bytes 6291472 | tf_op jit(solution)/shard_map/all_gather | solution.py:10
  163.5 384.0 %all-gather.5.cloned.1.call-done = bf16[4,688,4096]{2,1,0:T(8,128)(2,1)} async-done(((bf16[4,688,1024]{2,1,0:T(8,128)(2,1)}), bf16[4,688,4096]{2,1,0:T(8,128)(2,1)}) %all-gather.5.cloned.1.call-update) | async-done | bytes 22544400 | tf_op jit(solution)/shard_map/all_gather | solution.py:28
  547.5 22.8 %multiply_reduce_fusion = f32[4,768]{1,0:T(4,128)S(1)} fusion(f32[688,768]{1,0:T(8,128)S(1)} %fusion.4, bf16[4,688,4096]{2,1,0:T(8,128)(2,1)} %all-gather.5.cloned.1.call-done, bf16[768,4096]{1,0:T(8,128)(2,1)} %all-gather.9.cloned.1.call-done), kind=kOutput, calls=%fused_computation.1 | convolution fusion | flops 17318309888 | bytes 30961664 | tf_op jit(solution)/shard_map/td,qjd->qjt/dot_general | solution.py:25
  570.3 0.1 reduce_sum.18
  570.4 13.6 %psum.7 = f32[6,4]{0,1:T(4,128)S(1)} all-reduce(f32[6,4]{0,1:T(4,128)S(1)} %bitcast.15), channel_id=1, replica_groups=mesh['dp'=4,'tensor'=8] {'tensor'}, use_global_device_ids=true, to_apply=%region_2.3 | all-reduce | flops 24 | bytes 192 | tf_op jit(solution)/shard_map/psum | solution.py:33
  584.0 0.6 broadcast_multiply_fusion
  (1 shorter events, 0.0 us)
Async XLA Ops:
  6.5 52.0 %all-gather.7.cloned.1.call-start = ((), (), s32[]{:S(2)}) async-start(), calls=%async_computation.1 | async-start | bytes 7077888 | tf_op jit(solution)/shard_map/all_gather | solution.py:8
  7.3 107.7 %all-gather.11.cloned.1.call-start = ((), (), s32[]{:S(2)}) async-start(), calls=%async_computation.3 | async-start | bytes 9510912 | tf_op jit(solution)/shard_map/all_gather | solution.py:15
  8.0 59.6 %copy-start = (f32[688,1024]{1,0:T(8,128)S(1)}, f32[688,1024]{1,0:T(8,128)}, u32[]{:S(2)}) copy-start(f32[688,1024]{1,0:T(8,128)} %param.13) | copy-start | bytes 8454148
  8.0 155.5 %all-gather.9.cloned.1.call-start = ((), (), s32[]{:S(2)}) async-start(), calls=%async_computation.2 | async-start | bytes 7077888 | tf_op jit(solution)/shard_map/all_gather | solution.py:10
  66.9 480.6 %all-gather.5.cloned.1.call-start = ((), (), s32[]{:S(2)}) async-start(), calls=%async_computation | async-start | bytes 28180480 | tf_op jit(solution)/shard_map/all_gather | solution.py:28
  68.1 7.5 %copy-start.1 = (s32[6]{0:T(128)S(1)}, s32[6]{0:T(128)}, u32[]{:S(2)}) copy-start(s32[6]{0:T(128)} %param.15) | copy-start | bytes 76
Sparse Core Ops, SparseCore 0:
  9.2 49.2 all-gather.6
  60.4 54.5 all-gather.10
  116.9 46.5 all-gather.8
  164.9 382.4 all-gather.4
where the time goes:
time: 591 us
  waiting for transfers between devices  513 us (87%)
  matrix products  42 us (7%)
  between operations  13.8 us (2%)
  blocking collectives  13.6 us (2%)
  other arithmetic  8.66 us (1%)
    all_gather x1, waiting for transfers between devices, local(): lax.all_gather(scaled, 'dp', axis=2, tiled=True)  384 us
    all_gather x1, waiting for transfers between devices, local(): full_act = lax.all_gather(activations, 'tensor', axis=1, tiled=True)  50.5 us
    all_gather x1, waiting for transfers between devices, local(): lax.all_gather(out_grads_t, 'tensor', axis=0, tiled=True)  39.3 us
    all_gather x1, waiting for transfers between devices, local(): act_proj = lax.all_gather(act_local, 'tensor', axis=1, tiled=True)  37.6 us
    dot_general x1, matrix products, local(): jnp.einsum('td,qjd->qjt', act_proj, lax.all_gather(scaled, 'dp', axis=2,...  22.8 us
    psum x1, blocking collectives, local(): totals = lax.psum(partial_value, 'tensor')  13.6 us
  transfers between devices with their start and end apart: 4, of which 4 were waited for; matrix products, arithmetic and copies ran while one was open for 5% of the time, Pallas kernels for 0%

commit v1 on v0

--- a/solution.py
+++ b/solution.py
@@ -2,6 +2,22 @@
 import jax.numpy as jnp
 from jax import lax
 from jax.sharding import PartitionSpec as P
+
+
+def summed_both_ways(value, axis, dim, contribution):
+    count, place, rows = (lax.axis_size(axis), lax.axis_index(axis), value.shape[dim])
+    right = [(i, (i + 1) % count) for i in range(count)]
+    left = [(i, (i - 1) % count) for i in range(count)]
+    middle = count // 2
+    from_left = from_right = value
+    subtotal = contribution(value, place * rows)
+    for step in range(1, middle + 1):
+        from_left = lax.ppermute(from_left, axis, right)
+        if step < count - middle:
+            from_right = lax.ppermute(from_right, axis, left)
+            subtotal = subtotal + contribution(from_right, (place + step) % count * rows)
+        subtotal = subtotal + contribution(from_left, (place - step) % count * rows)
+    return subtotal
 
 
 def local(activations, out_grads_t, in_basis, out_basis_t, query_proj, eigvals, damping, lengths):
@@ -22,11 +38,16 @@
     grad_proj = (grad_full * keep).astype(jnp.bfloat16)
     scaled = (query_proj.astype(jnp.float32) / (eigvals + damping[0])).astype(jnp.bfloat16)
     query_count = query_proj.shape[0]
-    mixed = jnp.einsum(
-        "td,qjd->qjt",
-        act_proj,
-        lax.all_gather(scaled, "dp", axis=2, tiled=True),
-        preferred_element_type=jnp.float32,
+    mixed = summed_both_ways(
+        scaled,
+        "dp",
+        2,
+        lambda part, at: jnp.einsum(
+            "td,qjd->qjt",
+            lax.dynamic_slice_in_dim(act_proj, at, part.shape[2], axis=1),
+            part,
+            preferred_element_type=jnp.float32,
+        ),
     )
     weighted = mixed * grad_proj.astype(jnp.float32)[None, :, :]
     partial_value = jnp.sum(weighted.reshape(query_count, width, seq_count, seq_len), axis=(1, 3)).T

time: 591 us -> 479 us (0.81)
  waiting for transfers between devices: 513 us -> 375 us
  matrix products: 42 us -> 64.8 us
    all_gather x1 -> x0, waiting for transfers between devices: 384 us -> none  [local(): lax.all_gather(scaled, 'dp', axis=2, tiled=True)]
    ppermute x0 -> x3, waiting for transfers between devices: none -> 323 us  [the longest x2 235 us: summed_both_ways(): from_left = lax.ppermute(from_left, axis, right)]
    all_gather x1, waiting for transfers between devices: 39.3 us -> 0.01 us  [local(): lax.all_gather(out_grads_t, 'tensor', axis=0, tiled=True)]
    all_gather x1, waiting for transfers between devices: 37.6 us -> 0.02 us  [local(): act_proj = lax.all_gather(act_local, 'tensor', axis=1, tiled=True)]
    dot_general x1 -> x4, matrix products: 22.8 us -> 45.6 us  [local(): jnp.einsum('td,qjd->qjt', lax.dynamic_slice_in_dim(act_proj, at, part.sha...]
  transfers between devices with their start and end apart: 4 -> 6, of which waited for: 4 -> 4; matrix products, arithmetic and copies ran while one was open for 5% -> 12% of each run, Pallas kernels for 0% -> 0%
where the time goes in v1:
time: 479 us; the launch traced here: 478 us
  waiting for transfers between devices  375 us (78%)
  matrix products  64.8 us (14%)
  between operations  13.8 us (3%)
  blocking collectives  12.3 us (3%)
  other arithmetic  8.72 us (2%)
    ppermute x2, waiting for transfers between devices, summed_both_ways(): from_left = lax.ppermute(from_left, axis, right)  235 us
    ppermute x1, waiting for transfers between devices, summed_both_ways(): from_right = lax.ppermute(from_right, axis, left)  88.3 us
    all_gather x1, waiting for transfers between devices, local(): full_act = lax.all_gather(activations, 'tensor', axis=1, tiled=True)  50.5 us
    dot_general x4, matrix products, local(): jnp.einsum('td,qjd->qjt', lax.dynamic_slice_in_dim(act_proj, at, part.sha...  45.6 us
    psum x1, blocking collectives, local(): totals = lax.psum(partial_value, 'tensor')  12.3 us
    dot_general x1, matrix products, local(): jnp.dot(out_basis_t, lax.all_gather(out_grads_t, 'tensor', axis=0, tiled=...  10.9 us
  transfers between devices with their start and end apart: 6, of which 4 were waited for; matrix products, arithmetic and copies ran while one was open for 12% of the time, Pallas kernels for 0%

profile of v1, /device:TPU:0, one launch (start us, length us, event | category | flops | bytes accessed | tf_op | source)
XLA Modules:
  0.0 478.4 jit_solution(1382612305699786052)
XLA Ops:
  6.5 0.0 all-gather.4.cloned.1.call-start
  6.5 0.7 all-gather.4.cloned.1.call-update
  7.3 0.0 all-gather.8.cloned.1.call-start
  7.3 0.7 all-gather.8.cloned.1.call-update
  8.0 0.0 copy-start
  8.0 0.0 all-gather.6.cloned.1.call-start
  8.1 50.5 %all-gather.4.cloned.1.call-done = bf16[768,4096]{1,0:T(8,128)(2,1)} async-done(((bf16[768,512]{1,0:T(8,128)(2,1)}), bf16[768,4096]{1,0:T(8,128)(2,1)}) %all-gather.4.cloned.1.call-update) | async-done | bytes 6291472 | tf_op jit(solution)/shard_map/all_gather | solution.py:24
  58.5 8.3 %convolution_convert_fusion = bf16[768,512]{1,0:T(8,128)(2,1)} fusion(bf16[768,4096]{1,0:T(8,128)(2,1)} %all-gather.4.cloned.1.call-done, bf16[4096,512]{1,0:T(8,128)(2,1)} %param.10), kind=kOutput, calls=%fused_computation.16 | convolution fusion | flops 3221618688 | bytes 11272192 | tf_op jit(solution)/shard_map/dot_general | solution.py:25
  66.8 0.0 all-gather.6.cloned.1.call-update
  67.5 0.0 copy-done
  67.5 0.5 broadcast_add_fusion
  68.0 0.0 copy-start.1
  68.0 7.5 %divide_convert_fusion = bf16[4,688,1024]{2,1,0:T(8,128)(2,1)} fusion(bf16[4,688,1024]{2,1,0:T(8,128)(2,1)} %param.12, f32[688,1024]{1,0:T(8,128)S(1)} %broadcast_add_fusion), kind=kLoop, calls=%fused_computation | loop fusion | flops 8454144 | bytes 14090240 | tf_op jit(solution)/shard_map/convert_element_type | solution.py:39
  75.5 1.6 collective-permute-start.1
  77.1 2.2 collective-permute-start
  79.3 122.7 %collective-permute-done.1 = bf16[4,688,1024]{2,1,0:T(8,128)(2,1)} collective-permute-done((bf16[4,688,1024]{2,1,0:T(8,128)(2,1)}, bf16[4,688,1024]{2,1,0:T(8,128)(2,1)}, u32[]{:S(2)}, u32[]{:S(2)}) %collective-permute-start.1) | collective-permute-done | bytes 5636128 | tf_op jit(solution)/shard_map/ppermute | solution.py:15
  202.0 0.0 collective-permute-start.2
  202.0 0.0 copy-done.1
  202.0 0.1 convert_bitcast_fusion
  202.1 0.0 all-gather.8.cloned.1.call-done
  202.1 10.9 %fusion.11 = f32[688,768]{1,0:T(8,128)S(1)} fusion(bf16[688,5504]{1,0:T(8,128)(2,1)} %param.11, bf16[5504,768]{1,0:T(8,128)(2,1)} %all-gather.8.cloned.1.call-done, f32[768]{0:T(1024)S(1)} %convert_bitcast_fusion), kind=kOutput, calls=%fused_computation.14 | convolution fusion | flops 5818036224 | bytes 18144256 | tf_op jit(solution)/shard_map/dot_general | solution.py:29
  213.0 0.0 all-gather.6.cloned.1.call-done
  213.1 0.0 copy-start.2
  213.1 11.1 %fusion.1 = f32[4,688,768]{2,1,0:T(8,128)} fusion(bf16[4,688,1024]{2,1,0:T(8,128)(2,1)} %collective-permute-done.1, bf16[768,4096]{1,0:T(8,128)(2,1)} %all-gather.6.cloned.1.call-done, s32[]{:T(128)S(6)} %select_n.31), kind=kOutput, calls=%fused_computation.4 | convolution fusion | flops 4328521728 | bytes 15663108 | tf_op jit(solution)/shard_map/td,qjd->qjt/dot_general | solution.py:45
  224.1 0.0 copy-done.2
  224.1 9.2 %fusion.5 = f32[4,688,768]{2,1,0:T(8,128)} fusion(bf16[4,688,1024]{2,1,0:T(8,128)(2,1)} %divide_convert_fusion, bf16[768,4096]{1,0:T(8,128)(2,1)S(1)} %copy-done.2, s32[]{:T(128)S(6)} %select_n.27), kind=kOutput, calls=%fused_computation.8 | convolution fusion | flops 4328521728 | bytes 15663108 | tf_op jit(solution)/shard_map/td,qjd->qjt/dot_general | solution.py:45
  233.4 88.3 %collective-permute-done = bf16[4,688,1024]{2,1,0:T(8,128)(2,1)} collective-permute-done((bf16[4,688,1024]{2,1,0:T(8,128)(2,1)}, bf16[4,688,1024]{2,1,0:T(8,128)(2,1)}, u32[]{:S(2)}, u32[]{:S(2)}) %collective-permute-start) | collective-permute-done | bytes 5636128 | tf_op jit(solution)/shard_map/ppermute | solution.py:17
  321.6 9.3 %fusion.3 = f32[4,688,768]{2,1,0:T(8,128)} fusion(bf16[4,688,1024]{2,1,0:T(8,128)(2,1)} %collective-permute-done, bf16[768,4096]{1,0:T(8,128)(2,1)S(1)} %copy-done.2, s32[]{:T(128)S(6)} %select_n.29), kind=kOutput, calls=%fused_computation.6 | convolution fusion | flops 4328521728 | bytes 15663108 | tf_op jit(solution)/shard_map/td,qjd->qjt/dot_general | solution.py:45
  331.0 111.9 %collective-permute-done.2 = bf16[4,688,1024]{2,1,0:T(8,128)(2,1)} collective-permute-done((bf16[4,688,1024]{2,1,0:T(8,128)(2,1)}, bf16[4,688,1024]{2,1,0:T(8,128)(2,1)}, u32[]{:S(2)}, u32[]{:S(2)}) %collective-permute-start.2) | collective-permute-done | bytes 5636128 | tf_op jit(solution)/shard_map/ppermute | solution.py:15
  442.9 16.0 %multiply_reduce_fusion = f32[4,768]{1,0:T(4,128)S(1)} fusion(f32[4,688,768]{2,1,0:T(8,128)} %fusion.1, f32[4,688,768]{2,1,0:T(8,128)} %fusion.5, f32[4,688,768]{2,1,0:T(8,128)} %fusion.3, f32[688,768]{1,0:T(8,128)S(1)} %fusion.11, bf16[4,688,1024]{2,1,0:T(8,128)(2,1)} %collective-permute-done.2, bf16[768,4096]{1,0:T(8,128)(2,1)} %all-gather.6.cloned.1.call-done, ...), kind=kOutput, calls=%fused_computation.1 | convolution fusion | flops 4339086336 | bytes 34697220 | tf_op jit(solution)/shard_map/td,qjd->qjt/dot_general | solution.py:45
  458.9 0.1 reduce_sum.18
  459.0 12.3 %psum.7 = f32[6,4]{0,1:T(4,128)S(1)} all-reduce(f32[6,4]{0,1:T(4,128)S(1)} %bitcast.25), channel_id=1, replica_groups=mesh['dp'=4,'tensor'=8] {'tensor'}, use_global_device_ids=true, to_apply=%region_2.3 | all-reduce | flops 24 | bytes 192 | tf_op jit(solution)/shard_map/psum | solution.py:54
  471.2 0.6 broadcast_multiply_fusion
  (1 shorter events, 0.0 us)
Async XLA Ops:
  6.5 52.0 %all-gather.4.cloned.1.call-start = ((), (), s32[]{:S(2)}) async-start(), calls=%async_computation | async-start | bytes 7077888 | tf_op jit(solution)/shard_map/all_gather | solution.py:24
  7.3 194.9 %all-gather.8.cloned.1.call-start = ((), (), s32[]{:S(2)}) async-start(), calls=%async_computation.2 | async-start | bytes 9510912 | tf_op jit(solution)/shard_map/all_gather | solution.py:31
  8.0 59.5 %copy-start = (f32[688,1024]{1,0:T(8,128)S(1)}, f32[688,1024]{1,0:T(8,128)}, u32[]{:S(2)}) copy-start(f32[688,1024]{1,0:T(8,128)} %param.13) | copy-start | bytes 8454148
  8.0 205.0 %all-gather.6.cloned.1.call-start = ((), (), s32[]{:S(2)}) async-start(), calls=%async_computation.1 | async-start | bytes 7077888 | tf_op jit(solution)/shard_map/all_gather | solution.py:26
  68.0 134.0 %copy-start.1 = (s32[6]{0:T(128)S(1)}, s32[6]{0:T(128)}, u32[]{:S(2)}) copy-start(s32[6]{0:T(128)} %param.15) | copy-start | bytes 76
  75.5 126.5 %collective-permute-start.1 = (bf16[4,688,1024]{2,1,0:T(8,128)(2,1)}, bf16[4,688,1024]{2,1,0:T(8,128)(2,1)}, u32[]{:S(2)}, u32[]{:S(2)}) collective-permute-start(bf16[4,688,1024]{2,1,0:T(8,128)(2,1)} %divide_convert_fusion), channel_id=1, source_target_pairs={{0,8},{8,16},{16,24},{24,0},{1,9},{9,17},{17,25},{25,1},{2,10},{10... | collective-permute-start | bytes 16908296 | tf_op jit(solution)/shard_map/ppermute | solution.py:15
  77.1 244.5 %collective-permute-start = (bf16[4,688,1024]{2,1,0:T(8,128)(2,1)}, bf16[4,688,1024]{2,1,0:T(8,128)(2,1)}, u32[]{:S(2)}, u32[]{:S(2)}) collective-permute-start(bf16[4,688,1024]{2,1,0:T(8,128)(2,1)} %divide_convert_fusion), channel_id=1, source_target_pairs={{0,24},{8,0},{16,8},{24,16},{1,25},{9,1},{17,9},{25,17},{2,26},{10... | collective-permute-start | bytes 16908296 | tf_op jit(solution)/shard_map/ppermute | solution.py:17
  202.0 240.9 %collective-permute-start.2 = (bf16[4,688,1024]{2,1,0:T(8,128)(2,1)}, bf16[4,688,1024]{2,1,0:T(8,128)(2,1)}, u32[]{:S(2)}, u32[]{:S(2)}) collective-permute-start(bf16[4,688,1024]{2,1,0:T(8,128)(2,1)} %collective-permute-done.1), channel_id=1, source_target_pairs={{0,8},{8,16},{16,24},{24,0},{1,9},{9,17},{17,25},{25,1},{2,10},{10... | collective-permute-start | bytes 16908296 | tf_op jit(solution)/shard_map/ppermute | solution.py:15
  213.1 11.1 %copy-start.2 = (bf16[768,4096]{1,0:T(8,128)(2,1)S(1)}, bf16[768,4096]{1,0:T(8,128)(2,1)}, u32[]{:S(2)}) copy-start(bf16[768,4096]{1,0:T(8,128)(2,1)} %all-gather.6.cloned.1.call-done) | copy-start | bytes 18874372
Sparse Core Ops, SparseCore 0:
  9.2 49.2 all-gather.3
  60.4 54.5 all-gather.7
  116.9 46.5 all-gather.5
